TPU v7x, 128 devices: a whole 4x4x4 slice. The times are simulated.
128 devices in a mesh: row: 8 (over y, core), col: 16 (over x, z).
Axes of the slice: x: 4, y: 4, z: 4, core: 2. Of those that a mesh axis runs over, the one named last changes fastest.
Arguments:
- probes: bfloat16 [4, 32768, 256], P(None, ('row', 'col')), may hold values from -6 to 6
- points: bfloat16 [16, 4, 32768], P(None, None, ('row', 'col')), may hold values from -8 to 8
- leaf_skeleton: int32 [256, 64], P(('row', 'col')), may hold values from 0 to 127, as said below
- skeleton_one: int32 [128, 64], P(('row', 'col')), may hold values from 0 to 127, as said below
- skeleton_two: int32 [64, 64], P('row'), may hold values from 0 to 127, as said below
- skeleton_three: int32 [32, 64], P('row'), may hold values from 0 to 127, as said below
Outputs:
- leaf_interp: float32 [256, 128, 64], P(('row', 'col'))
- upper_interp: float32 [3, 128, 128, 64], P(None, ('row', 'col'))
- top_state: float32 [2, 128, 64, 256], P(None, ('row', 'col'))
Inputs may be any that keep to these rules, and one draw needn't show every extreme that they name: `leaf_skeleton`: each row names 64 different rows of its leaf, in ascending order. `skeleton_one`: each row names 64 different rows of the node's stacked child skeletons, in ascending order. `skeleton_two`: each row names 64 different rows of the node's stacked child skeletons, in ascending order. `skeleton_three`: each row names 64 different rows of the node's stacked child skeletons, in ascending order.
All inputs are finite; a program needn't handle non-finite values.
Results may differ from a plain program's by a relative error of at most 0.0059.
Values may be sent and summed in bfloat16 or wider, within the bound.
A program may use at most 64 MiB of HBM per device.

v0:
```python
from functools import partial
import math
import jax
import jax.numpy as jnp
from jax import lax
from jax.sharding import PartitionSpec as P

LEAF = 128
exact_mode = lax.Precision.HIGHEST


def swapped(value, axis, bit):
    return lax.ppermute(value, axis, [(i, i ^ 1 << bit) for i in range(lax.axis_size(axis))])


def couple(row_feats, col_feats, kernel_gain):
    cross = jnp.dot(row_feats.T, col_feats, precision=exact_mode)
    row_sq = jnp.sum(row_feats * row_feats, axis=0)
    col_sq = jnp.sum(col_feats * col_feats, axis=0)
    feat_count = row_feats.shape[0]
    return kernel_gain * jnp.exp(
        (2.0 * cross - row_sq[:, None] - col_sq[None, :]) / (2.0 * feat_count)
    )


def interpolate(stacked, chosen):
    skeleton = jnp.take(stacked, chosen, axis=0)
    gram_mat = jnp.dot(skeleton, skeleton.T, precision=exact_mode)
    damping = 0.05 * jnp.sum(skeleton * skeleton) / chosen.shape[0] + 1e-05
    factor = jnp.linalg.cholesky(gram_mat + damping * jnp.eye(chosen.shape[0], dtype=stacked.dtype))
    cross_mat = jnp.dot(stacked, skeleton.T, precision=exact_mode)
    solved = jax.scipy.linalg.cho_solve((factor, True), cross_mat.T)
    return (solved.T, skeleton)


def leaf_level(leaf_rows, leaf_probes, coords, chosen):
    interp, skeleton = interpolate(leaf_rows, chosen)
    reduced = jnp.dot(interp.T, leaf_probes.astype(interp.dtype), precision=exact_mode)
    picked = jnp.take(coords, chosen, axis=1).astype(jnp.float32)
    return (interp, (skeleton, reduced, picked))


def merge_pair(first_child, second_child, chosen, kernel_gain):
    first_samples, first_reduced, first_points = first_child
    second_samples, second_reduced, second_points = second_child
    upper_rows = first_samples - jnp.dot(
        couple(first_points, second_points, kernel_gain), second_reduced, precision=exact_mode
    )
    lower_rows = second_samples - jnp.dot(
        couple(second_points, first_points, kernel_gain), first_reduced, precision=exact_mode
    )
    stacked = jnp.concatenate([upper_rows, lower_rows], axis=0)
    interp, skeleton = interpolate(stacked, chosen)
    reduced = jnp.dot(
        interp.T, jnp.concatenate([first_reduced, second_reduced], axis=0), precision=exact_mode
    )
    joined = jnp.take(jnp.concatenate([first_points, second_points], axis=1), chosen, axis=1)
    return (interp, (skeleton, reduced, joined))


def take_first(values):
    return values[0]


def take_second(values):
    return values[1]


def local(probes, points, leaf_skeleton, skeleton_one, skeleton_two, skeleton_three):
    feat_count = points.shape[0]
    own_rows = probes.shape[1]
    row_count = lax.axis_size("row")
    col_count = lax.axis_size("col")
    row_pos = lax.axis_index("row")
    col_pos = lax.axis_index("col")
    row_span = own_rows * col_count
    extent = row_span * row_count
    kernel_gain = 16.0 / math.sqrt(4 * extent)
    probe_cols = lax.all_gather(probes, "row", axis=1, tiled=True).reshape(
        4 * row_count * own_rows, -1
    )
    row_coords = lax.all_gather(points[:, 0], "col", axis=1, tiled=True)
    col_coords = lax.all_gather(points, "row", axis=2, tiled=True).reshape(
        feat_count, 4 * row_count * own_rows
    )
    col_wide = col_coords.astype(jnp.float32)
    col_sq = jnp.sum(col_wide * col_wide, axis=0)
    row_leaf = (row_pos * row_span + jnp.arange(row_span, dtype=jnp.int32)) // LEAF
    quarter_len = row_count * own_rows
    offsets = jnp.arange(4 * quarter_len, dtype=jnp.int32)
    quarter = offsets // quarter_len
    within = offsets % quarter_len
    col_leaf = (
        quarter * extent + within // own_rows * row_span + col_pos * own_rows + within % own_rows
    ) // LEAF
    height = 512

    def one_block(first_row):
        coords = lax.dynamic_slice_in_dim(row_coords, first_row, height, 1)
        leaves = lax.dynamic_slice_in_dim(row_leaf, first_row, height, 0)
        cross = lax.dot_general(
            coords, col_coords, (((0,), (0,)), ((), ())), preferred_element_type=jnp.float32
        )
        row_wide = coords.astype(jnp.float32)
        row_sq = jnp.sum(row_wide * row_wide, axis=0)
        kernel_tile = kernel_gain * jnp.exp(
            (2.0 * cross - row_sq[:, None] - col_sq[None, :]) / (2.0 * feat_count)
        )
        kernel_tile = jnp.where(leaves[:, None] == col_leaf[None, :], 0.0, kernel_tile).astype(
            jnp.bfloat16
        )
        return jnp.dot(kernel_tile, probe_cols, preferred_element_type=jnp.float32)

    starts = jnp.arange(row_span // height, dtype=jnp.int32) * height
    summed = lax.psum(lax.map(one_block, starts).reshape(row_span, -1), "col")
    owned = lax.dynamic_slice_in_dim(summed, col_pos * own_rows, own_rows, 0)
    leaf_count = own_rows // LEAF
    leaf_rows = owned.reshape(leaf_count, LEAF, -1)
    leaf_probes = probes[0].reshape(leaf_count, LEAF, -1)
    leaf_coords = points[:, 0].reshape(feat_count, leaf_count, LEAF).transpose(1, 0, 2)
    leaf_interp, carried = jax.vmap(leaf_level)(leaf_rows, leaf_probes, leaf_coords, leaf_skeleton)
    first_child = jax.tree.map(take_first, carried)
    second_child = jax.tree.map(take_second, carried)
    interp_one, carried = merge_pair(first_child, second_child, skeleton_one[0], kernel_gain)
    upper_list = [interp_one]
    for bit_num in range(2):
        partner = swapped((carried[0], carried[1], carried[2]), "col", bit_num)
        mine_first = col_pos >> bit_num & 1 == 0
        first_child = jax.tree.map(partial(jnp.where, mine_first), carried, partner)
        second_child = jax.tree.map(partial(jnp.where, mine_first), partner, carried)
        table_rows = skeleton_two if bit_num == 0 else skeleton_three
        chosen = lax.dynamic_index_in_dim(table_rows, col_pos // (2 << bit_num), 0, keepdims=False)
        interp_up, carried = merge_pair(first_child, second_child, chosen, kernel_gain)
        upper_list.append(interp_up)
    upper_interp = jnp.stack(upper_list)[:, None]
    top_state = jnp.stack([carried[0], carried[1]])[:, None]
    return (leaf_interp, upper_interp, top_state)


def solution(mesh):
    placed = (
        P(None, ("row", "col"), None),
        P(None, None, ("row", "col")),
        P(("row", "col"), None),
        P(("row", "col"), None),
        P("row", None),
        P("row", None),
    )
    return jax.shard_map(
        local,
        mesh=mesh,
        in_specs=placed,
        out_specs=(
            P(("row", "col"), None, None),
            P(None, ("row", "col"), None, None),
            P(None, ("row", "col"), None, None),
        ),
        check_vma=False,
    )
```

profile of v0, /device:TPU:0, one launch (start us, length us, event | category | flops | bytes accessed | tf_op | source)
XLA Modules:
  0.0 333.6 jit_solution(17776641699340166567)
XLA Ops:
  8.7 12.7 %all_gather.10 = bf16[16,4,2048]{2,1,0:T(4,128)(2,1)S(1)} all-gather(bf16[16,4,256]{2,1,0:T(4,128)(2,1)} %param.16), channel_id=1, replica_groups=mesh['row'=8,'col'=16] {'row'}, dimensions={2}, use_global_device_ids=true | all-gather | bytes 294912 | tf_op jit(solution)/shard_map/all_gather | solution.py:83
  21.8 25.1 %all-gather = bf16[16,1,4096]{2,0,1:T(8,128)(2,1)S(1)} all-gather(bf16[16,1,256]{2,0,1:T(8,128)(2,1)S(1)} %copy.60), channel_id=2, replica_groups=mesh['row'=8,'col'=16] {'col'}, dimensions={2}, use_global_device_ids=true | all-gather | bytes 139264 | tf_op jit(solution)/shard_map/all_gather | solution.py:82
  46.9 88.3 %while.11 = (s32[]{:T(128)}, f32[8,512,256]{2,1,0:T(8,128)}, s32[8]{0:T(128)S(1)}, s32[4096]{0:T(1024)S(1)}, bf16[16,4096]{1,0:T(8,128)(2,1)S(1)}, /*index=5*/bf...) while((s32[]{:T(128)}, f32[8,512,256]{2,1,0:T(8,128)}, ...), condition=%wide.region_3.4_spmd.clone, body=%wide.region_1.3_spmd.clone.sunk | while | flops 2315697664 | bytes 5122239 | solution.py:115
  49.7 8.3 %fusion.176 = f32[8,512,256]{2,1,0:T(8,128)} fusion(f32[8,512,256]{2,1,0:T(8,128)} %get-tuple-element.213, s32[]{:T(128)S(6)} %copy.67, bf16[8192,256]{1,0:T(8,128)(2,1)} %get-tuple-element.231, bf16[16,8192]{1,0:T(8,128)(2,1)S(1)} %get-tuple-element.229, f32[8192]{0:T(1024)S(1)} %get-tuple-element.230, f32[512]{0:T(512)S(1)} %multiply_reduce_fusion.13, ...), kind=kOutput, calls=%fused_computation.11.clone.1 | convolution fusion | flops 2315255808 | bytes 5066760 | tf_op jit(solution)/shard_map/while/body/eval_jaxpr/dot_general | solution.py:112
  60.7 8.3 %fusion.176 = f32[8,512,256]{2,1,0:T(8,128)} fusion(f32[8,512,256]{2,1,0:T(8,128)} %get-tuple-element.213, s32[]{:T(128)S(6)} %copy.67, bf16[8192,256]{1,0:T(8,128)(2,1)} %get-tuple-element.231, bf16[16,8192]{1,0:T(8,128)(2,1)S(1)} %get-tuple-element.229, f32[8192]{0:T(1024)S(1)} %get-tuple-element.230, f32[512]{0:T(512)S(1)} %multiply_reduce_fusion.13, ...), kind=kOutput, calls=%fused_computation.11.clone.1 | convolution fusion | flops 2315255808 | bytes 5066760 | tf_op jit(solution)/shard_map/while/body/eval_jaxpr/dot_general | solution.py:112
  71.8 8.3 %fusion.176 = f32[8,512,256]{2,1,0:T(8,128)} fusion(f32[8,512,256]{2,1,0:T(8,128)} %get-tuple-element.213, s32[]{:T(128)S(6)} %copy.67, bf16[8192,256]{1,0:T(8,128)(2,1)} %get-tuple-element.231, bf16[16,8192]{1,0:T(8,128)(2,1)S(1)} %get-tuple-element.229, f32[8192]{0:T(1024)S(1)} %get-tuple-element.230, f32[512]{0:T(512)S(1)} %multiply_reduce_fusion.13, ...), kind=kOutput, calls=%fused_computation.11.clone.1 | convolution fusion | flops 2315255808 | bytes 5066760 | tf_op jit(solution)/shard_map/while/body/eval_jaxpr/dot_general | solution.py:112
  82.8 8.3 %fusion.176 = f32[8,512,256]{2,1,0:T(8,128)} fusion(f32[8,512,256]{2,1,0:T(8,128)} %get-tuple-element.213, s32[]{:T(128)S(6)} %copy.67, bf16[8192,256]{1,0:T(8,128)(2,1)} %get-tuple-element.231, bf16[16,8192]{1,0:T(8,128)(2,1)S(1)} %get-tuple-element.229, f32[8192]{0:T(1024)S(1)} %get-tuple-element.230, f32[512]{0:T(512)S(1)} %multiply_reduce_fusion.13, ...), kind=kOutput, calls=%fused_computation.11.clone.1 | convolution fusion | flops 2315255808 | bytes 5066760 | tf_op jit(solution)/shard_map/while/body/eval_jaxpr/dot_general | solution.py:112
  93.9 8.3 %fusion.176 = f32[8,512,256]{2,1,0:T(8,128)} fusion(f32[8,512,256]{2,1,0:T(8,128)} %get-tuple-element.213, s32[]{:T(128)S(6)} %copy.67, bf16[8192,256]{1,0:T(8,128)(2,1)} %get-tuple-element.231, bf16[16,8192]{1,0:T(8,128)(2,1)S(1)} %get-tuple-element.229, f32[8192]{0:T(1024)S(1)} %get-tuple-element.230, f32[512]{0:T(512)S(1)} %multiply_reduce_fusion.13, ...), kind=kOutput, calls=%fused_computation.11.clone.1 | convolution fusion | flops 2315255808 | bytes 5066760 | tf_op jit(solution)/shard_map/while/body/eval_jaxpr/dot_general | solution.py:112
  104.9 8.3 %fusion.176 = f32[8,512,256]{2,1,0:T(8,128)} fusion(f32[8,512,256]{2,1,0:T(8,128)} %get-tuple-element.213, s32[]{:T(128)S(6)} %copy.67, bf16[8192,256]{1,0:T(8,128)(2,1)} %get-tuple-element.231, bf16[16,8192]{1,0:T(8,128)(2,1)S(1)} %get-tuple-element.229, f32[8192]{0:T(1024)S(1)} %get-tuple-element.230, f32[512]{0:T(512)S(1)} %multiply_reduce_fusion.13, ...), kind=kOutput, calls=%fused_computation.11.clone.1 | convolution fusion | flops 2315255808 | bytes 5066760 | tf_op jit(solution)/shard_map/while/body/eval_jaxpr/dot_general | solution.py:112
  116.0 8.3 %fusion.176 = f32[8,512,256]{2,1,0:T(8,128)} fusion(f32[8,512,256]{2,1,0:T(8,128)} %get-tuple-element.213, s32[]{:T(128)S(6)} %copy.67, bf16[8192,256]{1,0:T(8,128)(2,1)} %get-tuple-element.231, bf16[16,8192]{1,0:T(8,128)(2,1)S(1)} %get-tuple-element.229, f32[8192]{0:T(1024)S(1)} %get-tuple-element.230, f32[512]{0:T(512)S(1)} %multiply_reduce_fusion.13, ...), kind=kOutput, calls=%fused_computation.11.clone.1 | convolution fusion | flops 2315255808 | bytes 5066760 | tf_op jit(solution)/shard_map/while/body/eval_jaxpr/dot_general | solution.py:112
  127.0 8.3 %fusion.176 = f32[8,512,256]{2,1,0:T(8,128)} fusion(f32[8,512,256]{2,1,0:T(8,128)} %get-tuple-element.213, s32[]{:T(128)S(6)} %copy.67, bf16[8192,256]{1,0:T(8,128)(2,1)} %get-tuple-element.231, bf16[16,8192]{1,0:T(8,128)(2,1)S(1)} %get-tuple-element.229, f32[8192]{0:T(1024)S(1)} %get-tuple-element.230, f32[512]{0:T(512)S(1)} %multiply_reduce_fusion.13, ...), kind=kOutput, calls=%fused_computation.11.clone.1 | convolution fusion | flops 2315255808 | bytes 5066760 | tf_op jit(solution)/shard_map/while/body/eval_jaxpr/dot_general | solution.py:112
  136.2 1.1 gather_fusion.1
  138.3 1.3 collective-permute-start.1
  143.1 2.5 collective-permute-start.4
  146.1 3.6 %collective-permute-done.4 = f32[16,64]{0,1:T(8,128)S(1)} collective-permute-done((f32[16,64]{0,1:T(8,128)S(1)}, f32[16,64]{0,1:T(8,128)S(1)}, u32[]{:S(2)}, u32[]{:S(2)}) %collective-permute-start.4) | collective-permute-done | bytes 4128 | tf_op jit(solution)/shard_map/ppermute | solution.py:13
  149.8 87.9 %all-reduce.2.cloned.1.call-done = f32[4096,256]{1,0:T(8,128)} async-done(((f32[4096,256]{1,0:T(8,128)}), f32[4096,256]{1,0:T(8,128)}) %all-reduce.2.cloned.1.call-update) | async-done | bytes 4194320 | tf_op jit(solution)/shard_map/psum | solution.py:115
  237.7 1.0 constant_dynamic-slice_fusion.2
  238.7 1.3 gather_fusion
  241.0 11.7 %custom-call.18 = f32[2,64,64]{2,1,0:T(8,128)S(1)} custom-call(f32[2,64,64]{2,1,0:T(8,128)S(1)} %fusion.80), custom_call_target="Cholesky" | custom-call | tf_op jit(solution)/shard_map/vmap(jit(cholesky))/cholesky | solution.py:30
  253.0 9.8 %custom-call.19 = f32[2,1,64,64]{2,3,1,0:T(8,128)S(1)} custom-call(f32[2,1,64,64]{3,2,1,0:T(8,128)S(1)} %select_bitcast_fusion), custom_call_target="InvertDiagBlocksLowerTriangular" | custom-call | tf_op jit(solution)/shard_map/vmap(jit(_cho_solve))/triangular_solve | solution.py:32
  266.6 5.8 %cholesky.106 = f32[64,64]{1,0:T(8,128)S(1)} custom-call(f32[64,64]{1,0:T(8,128)S(1)} %fusion.101), custom_call_target="Cholesky" | custom-call | tf_op jit(solution)/shard_map/jit(cholesky)/cholesky | solution.py:30
  273.8 4.9 %custom-call.26 = f32[1,64,64]{1,2,0:T(8,128)S(1)} custom-call(f32[1,64,64]{2,1,0:T(8,128)S(1)} %fusion.84), custom_call_target="InvertDiagBlocksLowerTriangular" | custom-call | tf_op jit(solution)/shard_map/jit(_cho_solve)/triangular_solve | solution.py:32
  279.3 1.3 collective-permute-start.2
  281.7 2.5 collective-permute-done.2
  287.9 5.8 %cholesky.117 = f32[64,64]{1,0:T(8,128)S(1)} custom-call(f32[64,64]{1,0:T(8,128)S(1)} %fusion.96), custom_call_target="Cholesky" | custom-call | tf_op jit(solution)/shard_map/jit(cholesky)/cholesky | solution.py:30
  295.1 4.9 %custom-call.27 = f32[1,64,64]{1,2,0:T(8,128)S(1)} custom-call(f32[1,64,64]{2,1,0:T(8,128)S(1)} %fusion.85), custom_call_target="InvertDiagBlocksLowerTriangular" | custom-call | tf_op jit(solution)/shard_map/jit(_cho_solve)/triangular_solve | solution.py:32
  300.6 2.9 collective-permute-start.5
  303.8 1.0 collective-permute-start.3
  304.7 1.7 collective-permute-done.5
  306.7 3.1 collective-permute-done.3
  312.7 5.8 %cholesky.128 = f32[64,64]{1,0:T(8,128)S(1)} custom-call(f32[64,64]{1,0:T(8,128)S(1)} %fusion.91), custom_call_target="Cholesky" | custom-call | tf_op jit(solution)/shard_map/jit(cholesky)/cholesky | solution.py:30
  319.9 4.9 %custom-call.28 = f32[1,64,64]{1,2,0:T(8,128)S(1)} custom-call(f32[1,64,64]{2,1,0:T(8,128)S(1)} %fusion.86), custom_call_target="InvertDiagBlocksLowerTriangular" | custom-call | tf_op jit(solution)/shard_map/jit(_cho_solve)/triangular_solve | solution.py:32
  (152 shorter events, 32.3 us)
Async XLA Ops:
  7.2 39.8 %all-gather.3.cloned.1.call-start = ((), (), s32[]{:S(2)}) async-start(), calls=%async_computation | async-start | bytes 4718592 | tf_op jit(solution)/shard_map/all_gather | solution.py:79
  7.9 229.8 %all-reduce.2.cloned.1.call-start = ((), (), s32[]{:S(2)}) async-start(), calls=%async_computation.1 | async-start | bytes 8388608 | tf_op jit(solution)/shard_map/psum | solution.py:115
  135.3 0.7 copy-start.1
  135.3 2.3 copy-start.2
  138.3 4.0 %collective-permute-start.1 = (f32[16,64]{0,1:T(8,128)S(1)}, f32[16,64]{0,1:T(8,128)S(1)}, u32[]{:S(2)}, u32[]{:S(2)}) collective-permute-start(f32[16,64]{0,1:T(8,128)S(1)} %select_bitcast_fusion.3), channel_id=1, source_target_pairs={{0,1},{1,0},{2,3},{3,2},{4,5},{5,4},{6,7},{7,6},{8,9},{9,8},{10,11... | collective-permute-start | bytes 12296 | tf_op jit(solution)/shard_map/ppermute | solution.py:13
  143.1 6.5 %collective-permute-start.4 = (f32[16,64]{0,1:T(8,128)S(1)}, f32[16,64]{0,1:T(8,128)S(1)}, u32[]{:S(2)}, u32[]{:S(2)}) collective-permute-start(f32[16,64]{0,1:T(8,128)S(1)} %select_bitcast_fusion.2), channel_id=1, source_target_pairs={{0,2},{1,3},{2,0},{3,1},{4,6},{5,7},{6,4},{7,5},{8,10},{9,11},{10,... | collective-permute-start | bytes 12296 | tf_op jit(solution)/shard_map/ppermute | solution.py:13
  263.3 49.3 %copy-start = (f32[2,64,128]{2,1,0:T(8,128)}, f32[2,64,128]{2,1,0:T(8,128)S(1)}, u32[]{:S(2)}) copy-start(f32[2,64,128]{2,1,0:T(8,128)S(1)} %fusion.75) | copy-start | bytes 196612
  279.3 4.9 %collective-permute-start.2 = (f32[64,256]{1,0:T(8,128)S(1)}, f32[64,256]{1,0:T(8,128)S(1)}, u32[]{:S(2)}, u32[]{:S(2)}) collective-permute-start(f32[64,256]{1,0:T(8,128)S(1)} %fusion.64), channel_id=1, source_target_pairs={{0,1},{1,0},{2,3},{3,2},{4,5},{5,4},{6,7},{7,6},{8,9},{9,8},{10,11... | collective-permute-start | bytes 196616 | tf_op jit(solution)/shard_map/ppermute | solution.py:13
  280.8 4.3 %collective-permute-start = (f32[64,256]{1,0:T(8,128)S(1)}, f32[64,256]{1,0:T(8,128)S(1)}, u32[]{:S(2)}, u32[]{:S(2)}) collective-permute-start(f32[64,256]{1,0:T(8,128)S(1)} %get-tuple-element.110), channel_id=1, source_target_pairs={{0,1},{1,0},{2,3},{3,2},{4,5},{5,4},{6,7},{7,6},{8,9},{9,8},{10,11... | collective-permute-start | bytes 196616 | tf_op jit(solution)/shard_map/ppermute | solution.py:13
  300.6 5.8 %collective-permute-start.5 = (f32[64,256]{1,0:T(8,128)S(1)}, f32[64,256]{1,0:T(8,128)S(1)}, u32[]{:S(2)}, u32[]{:S(2)}) collective-permute-start(f32[64,256]{1,0:T(8,128)S(1)} %fusion.68), channel_id=1, source_target_pairs={{0,2},{1,3},{2,0},{3,1},{4,6},{5,7},{6,4},{7,5},{8,10},{9,11},{10,... | collective-permute-start | bytes 196616 | tf_op jit(solution)/shard_map/ppermute | solution.py:13
  303.8 6.1 %collective-permute-start.3 = (f32[64,256]{1,0:T(8,128)S(1)}, f32[64,256]{1,0:T(8,128)S(1)}, u32[]{:S(2)}, u32[]{:S(2)}) collective-permute-start(f32[64,256]{1,0:T(8,128)S(1)} %get-tuple-element.108), channel_id=1, source_target_pairs={{0,2},{1,3},{2,0},{3,1},{4,6},{5,7},{6,4},{7,5},{8,10},{9,11},{10,... | collective-permute-start | bytes 196616 | tf_op jit(solution)/shard_map/ppermute | solution.py:13
Sparse Core Ops, SparseCore 0:
  9.7 34.5 all-gather.2
  135.4 102.2 all-reduce.1
where the time goes:
time: 334 us
  waiting for transfers between devices  101 us (30%)
  matrix products  73.3 us (22%)
  other arithmetic  64.5 us (19%)
  blocking collectives  37.8 us (11%)
  between operations  16.6 us (5%)
  loops' own time  15.6 us (5%)
  local copies, waits for them, and re-layouts  15.3 us (5%)
  starting transfers between devices  9.94 us (3%)
    psum x1, waiting for transfers between devices, local(): summed = lax.psum(lax.map(one_block, starts).reshape(row_span, -1), 'col')  87.9 us
    dot_general x8, matrix products, one_block(): return jnp.dot(kernel_tile, probe_cols, preferred_element_type=jnp.float32)  66.3 us
    another operation x13, other arithmetic, interpolate(): jnp.linalg.cholesky(gram_mat + damping * jnp.eye(chosen.shape[0], dtype=s...  31.4 us
    another operation x9, other arithmetic, interpolate(): solved = jax.scipy.linalg.cho_solve((factor, True), cross_mat.T)  26.6 us
    all_gather x1, blocking collectives, local(): row_coords = lax.all_gather(points[:, 0], 'col', axis=1, tiled=True)  25.1 us
    another operation x1, loops' own time, local(): summed = lax.psum(lax.map(one_block, starts).reshape(row_span, -1), 'col')  15.6 us
    all_gather x1, blocking collectives, local(): lax.all_gather(points, 'row', axis=2, tiled=True)  12.7 us
    ppermute x6, waiting for transfers between devices, swapped(): lax.ppermute(value, axis, [(i, i ^ 1 << bit) for i in range(lax.axis_size...  12 us
  transfers between devices with their start and end apart: 8, of which 7 were waited for; matrix products, arithmetic and copies ran while one was open for 2% of the time, Pallas kernels for 0%

commit v1 on v0

--- a/solution.py
+++ b/solution.py
@@ -79,7 +79,7 @@
     probe_cols = lax.all_gather(probes, "row", axis=1, tiled=True).reshape(
         4 * row_count * own_rows, -1
     )
-    row_coords = lax.all_gather(points[:, 0], "col", axis=1, tiled=True)
+    row_coords = jnp.concatenate(lax.all_gather(points[:, 0], "col"), axis=1)
     col_coords = lax.all_gather(points, "row", axis=2, tiled=True).reshape(
         feat_count, 4 * row_count * own_rows
     )

time: 334 us -> 336 us (level)
  no operation moved by 1% of the time
where the time goes in v1:
time: 336 us; the launch traced here: 335 us
  waiting for transfers between devices  101 us (30%)
  matrix products  73.3 us (22%)
  other arithmetic  64.5 us (19%)
  blocking collectives  38.8 us (12%)
  between operations  16.6 us (5%)
  loops' own time  15.6 us (5%)
  local copies, waits for them, and re-layouts  15.3 us (5%)
  starting transfers between devices  10.3 us (3%)
    psum x1, waiting for transfers between devices, local(): summed = lax.psum(lax.map(one_block, starts).reshape(row_span, -1), 'col')  88.6 us
    dot_general x8, matrix products, one_block(): return jnp.dot(kernel_tile, probe_cols, preferred_element_type=jnp.float32)  66.3 us
    another operation x13, other arithmetic, interpolate(): jnp.linalg.cholesky(gram_mat + damping * jnp.eye(chosen.shape[0], dtype=s...  31.4 us
    another operation x9, other arithmetic, interpolate(): solved = jax.scipy.linalg.cho_solve((factor, True), cross_mat.T)  26.6 us
    all_gather x1, blocking collectives, local(): row_coords = jnp.concatenate(lax.all_gather(points[:, 0], 'col'), axis=1)  25.2 us
    another operation x1, loops' own time, local(): summed = lax.psum(lax.map(one_block, starts).reshape(row_span, -1), 'col')  15.6 us
    all_gather x1, blocking collectives, local(): lax.all_gather(points, 'row', axis=2, tiled=True)  13.7 us
    ppermute x6, waiting for transfers between devices, swapped(): lax.ppermute(value, axis, [(i, i ^ 1 << bit) for i in range(lax.axis_size...  11.5 us
  transfers between devices with their start and end apart: 8, of which 7 were waited for; matrix products, arithmetic and copies ran while one was open for 2% of the time, Pallas kernels for 0%

profile of v1, /device:TPU:0, one launch (start us, length us, event | category | flops | bytes accessed | tf_op | source)
XLA Modules:
  0.0 335.2 jit_solution(2079729645228889725)
XLA Ops:
  8.7 25.2 %all-gather = bf16[256,1,256]{2,0,1:T(8,128)(2,1)S(1)} all-gather(bf16[16,1,256]{2,0,1:T(8,128)(2,1)S(1)} %copy.91), channel_id=2, replica_groups=mesh['row'=8,'col'=16] {'col'}, dimensions={0}, use_global_device_ids=true | all-gather | bytes 139264 | tf_op jit(solution)/shard_map/all_gather | solution.py:82
  33.9 13.7 %all_gather.10 = bf16[16,4,2048]{2,1,0:T(4,128)(2,1)S(1)} all-gather(bf16[16,4,256]{2,1,0:T(4,128)(2,1)} %param.16), channel_id=1, replica_groups=mesh['row'=8,'col'=16] {'row'}, dimensions={2}, use_global_device_ids=true | all-gather | bytes 294912 | tf_op jit(solution)/shard_map/all_gather | solution.py:83
  48.0 88.3 %while.11 = (s32[]{:T(128)}, f32[8,512,256]{2,1,0:T(8,128)}, s32[8]{0:T(128)S(1)}, s32[4096]{0:T(1024)S(1)}, bf16[16,4096]{1,0:T(8,128)(2,1)S(1)}, /*index=5*/bf...) while((s32[]{:T(128)}, f32[8,512,256]{2,1,0:T(8,128)}, ...), condition=%wide.region_3.4_spmd.clone, body=%wide.region_1.3_spmd.clone.sunk | while | flops 2315697664 | bytes 5122239 | solution.py:115
  50.8 8.3 %fusion.176 = f32[8,512,256]{2,1,0:T(8,128)} fusion(f32[8,512,256]{2,1,0:T(8,128)} %get-tuple-element.219, s32[]{:T(128)S(6)} %copy.99, bf16[8192,256]{1,0:T(8,128)(2,1)} %get-tuple-element.237, bf16[16,8192]{1,0:T(8,128)(2,1)S(1)} %get-tuple-element.235, f32[8192]{0:T(1024)S(1)} %get-tuple-element.236, f32[512]{0:T(512)S(1)} %multiply_reduce_fusion.13, ...), kind=kOutput, calls=%fused_computation.11.clone.1 | convolution fusion | flops 2315255808 | bytes 5066760 | tf_op jit(solution)/shard_map/while/body/eval_jaxpr/dot_general | solution.py:112
  61.8 8.3 %fusion.176 = f32[8,512,256]{2,1,0:T(8,128)} fusion(f32[8,512,256]{2,1,0:T(8,128)} %get-tuple-element.219, s32[]{:T(128)S(6)} %copy.99, bf16[8192,256]{1,0:T(8,128)(2,1)} %get-tuple-element.237, bf16[16,8192]{1,0:T(8,128)(2,1)S(1)} %get-tuple-element.235, f32[8192]{0:T(1024)S(1)} %get-tuple-element.236, f32[512]{0:T(512)S(1)} %multiply_reduce_fusion.13, ...), kind=kOutput, calls=%fused_computation.11.clone.1 | convolution fusion | flops 2315255808 | bytes 5066760 | tf_op jit(solution)/shard_map/while/body/eval_jaxpr/dot_general | solution.py:112
  72.8 8.3 %fusion.176 = f32[8,512,256]{2,1,0:T(8,128)} fusion(f32[8,512,256]{2,1,0:T(8,128)} %get-tuple-element.219, s32[]{:T(128)S(6)} %copy.99, bf16[8192,256]{1,0:T(8,128)(2,1)} %get-tuple-element.237, bf16[16,8192]{1,0:T(8,128)(2,1)S(1)} %get-tuple-element.235, f32[8192]{0:T(1024)S(1)} %get-tuple-element.236, f32[512]{0:T(512)S(1)} %multiply_reduce_fusion.13, ...), kind=kOutput, calls=%fused_computation.11.clone.1 | convolution fusion | flops 2315255808 | bytes 5066760 | tf_op jit(solution)/shard_map/while/body/eval_jaxpr/dot_general | solution.py:112
  83.9 8.3 %fusion.176 = f32[8,512,256]{2,1,0:T(8,128)} fusion(f32[8,512,256]{2,1,0:T(8,128)} %get-tuple-element.219, s32[]{:T(128)S(6)} %copy.99, bf16[8192,256]{1,0:T(8,128)(2,1)} %get-tuple-element.237, bf16[16,8192]{1,0:T(8,128)(2,1)S(1)} %get-tuple-element.235, f32[8192]{0:T(1024)S(1)} %get-tuple-element.236, f32[512]{0:T(512)S(1)} %multiply_reduce_fusion.13, ...), kind=kOutput, calls=%fused_computation.11.clone.1 | convolution fusion | flops 2315255808 | bytes 5066760 | tf_op jit(solution)/shard_map/while/body/eval_jaxpr/dot_general | solution.py:112
  94.9 8.3 %fusion.176 = f32[8,512,256]{2,1,0:T(8,128)} fusion(f32[8,512,256]{2,1,0:T(8,128)} %get-tuple-element.219, s32[]{:T(128)S(6)} %copy.99, bf16[8192,256]{1,0:T(8,128)(2,1)} %get-tuple-element.237, bf16[16,8192]{1,0:T(8,128)(2,1)S(1)} %get-tuple-element.235, f32[8192]{0:T(1024)S(1)} %get-tuple-element.236, f32[512]{0:T(512)S(1)} %multiply_reduce_fusion.13, ...), kind=kOutput, calls=%fused_computation.11.clone.1 | convolution fusion | flops 2315255808 | bytes 5066760 | tf_op jit(solution)/shard_map/while/body/eval_jaxpr/dot_general | solution.py:112
  106.0 8.3 %fusion.176 = f32[8,512,256]{2,1,0:T(8,128)} fusion(f32[8,512,256]{2,1,0:T(8,128)} %get-tuple-element.219, s32[]{:T(128)S(6)} %copy.99, bf16[8192,256]{1,0:T(8,128)(2,1)} %get-tuple-element.237, bf16[16,8192]{1,0:T(8,128)(2,1)S(1)} %get-tuple-element.235, f32[8192]{0:T(1024)S(1)} %get-tuple-element.236, f32[512]{0:T(512)S(1)} %multiply_reduce_fusion.13, ...), kind=kOutput, calls=%fused_computation.11.clone.1 | convolution fusion | flops 2315255808 | bytes 5066760 | tf_op jit(solution)/shard_map/while/body/eval_jaxpr/dot_general | solution.py:112
  117.0 8.3 %fusion.176 = f32[8,512,256]{2,1,0:T(8,128)} fusion(f32[8,512,256]{2,1,0:T(8,128)} %get-tuple-element.219, s32[]{:T(128)S(6)} %copy.99, bf16[8192,256]{1,0:T(8,128)(2,1)} %get-tuple-element.237, bf16[16,8192]{1,0:T(8,128)(2,1)S(1)} %get-tuple-element.235, f32[8192]{0:T(1024)S(1)} %get-tuple-element.236, f32[512]{0:T(512)S(1)} %multiply_reduce_fusion.13, ...), kind=kOutput, calls=%fused_computation.11.clone.1 | convolution fusion | flops 2315255808 | bytes 5066760 | tf_op jit(solution)/shard_map/while/body/eval_jaxpr/dot_general | solution.py:112
  128.0 8.3 %fusion.176 = f32[8,512,256]{2,1,0:T(8,128)} fusion(f32[8,512,256]{2,1,0:T(8,128)} %get-tuple-element.219, s32[]{:T(128)S(6)} %copy.99, bf16[8192,256]{1,0:T(8,128)(2,1)} %get-tuple-element.237, bf16[16,8192]{1,0:T(8,128)(2,1)S(1)} %get-tuple-element.235, f32[8192]{0:T(1024)S(1)} %get-tuple-element.236, f32[512]{0:T(512)S(1)} %multiply_reduce_fusion.13, ...), kind=kOutput, calls=%fused_computation.11.clone.1 | convolution fusion | flops 2315255808 | bytes 5066760 | tf_op jit(solution)/shard_map/while/body/eval_jaxpr/dot_general | solution.py:112
  137.2 1.1 gather_fusion.1
  139.4 1.4 collective-permute-start.1
  144.2 2.8 collective-permute-start.4
  147.4 3.2 collective-permute-done.4
  150.7 88.6 %all-reduce.2.cloned.1.call-done = f32[4096,256]{1,0:T(8,128)} async-done(((f32[4096,256]{1,0:T(8,128)}), f32[4096,256]{1,0:T(8,128)}) %all-reduce.2.cloned.1.call-update) | async-done | bytes 4194320 | tf_op jit(solution)/shard_map/psum | solution.py:115
  239.4 1.0 constant_dynamic-slice_fusion.2
  240.3 1.3 gather_fusion
  242.7 11.7 %custom-call.18 = f32[2,64,64]{2,1,0:T(8,128)S(1)} custom-call(f32[2,64,64]{2,1,0:T(8,128)S(1)} %fusion.80), custom_call_target="Cholesky" | custom-call | tf_op jit(solution)/shard_map/vmap(jit(cholesky))/cholesky | solution.py:30
  254.6 9.8 %custom-call.19 = f32[2,1,64,64]{2,3,1,0:T(8,128)S(1)} custom-call(f32[2,1,64,64]{3,2,1,0:T(8,128)S(1)} %select_bitcast_fusion), custom_call_target="InvertDiagBlocksLowerTriangular" | custom-call | tf_op jit(solution)/shard_map/vmap(jit(_cho_solve))/triangular_solve | solution.py:32
  268.2 5.8 %cholesky.106 = f32[64,64]{1,0:T(8,128)S(1)} custom-call(f32[64,64]{1,0:T(8,128)S(1)} %fusion.101), custom_call_target="Cholesky" | custom-call | tf_op jit(solution)/shard_map/jit(cholesky)/cholesky | solution.py:30
  275.4 4.9 %custom-call.26 = f32[1,64,64]{1,2,0:T(8,128)S(1)} custom-call(f32[1,64,64]{2,1,0:T(8,128)S(1)} %fusion.84), custom_call_target="InvertDiagBlocksLowerTriangular" | custom-call | tf_op jit(solution)/shard_map/jit(_cho_solve)/triangular_solve | solution.py:32
  280.9 1.3 collective-permute-start.2
  283.3 2.5 collective-permute-done.2
  289.5 5.8 %cholesky.117 = f32[64,64]{1,0:T(8,128)S(1)} custom-call(f32[64,64]{1,0:T(8,128)S(1)} %fusion.96), custom_call_target="Cholesky" | custom-call | tf_op jit(solution)/shard_map/jit(cholesky)/cholesky | solution.py:30
  296.7 4.9 %custom-call.27 = f32[1,64,64]{1,2,0:T(8,128)S(1)} custom-call(f32[1,64,64]{2,1,0:T(8,128)S(1)} %fusion.85), custom_call_target="InvertDiagBlocksLowerTriangular" | custom-call | tf_op jit(solution)/shard_map/jit(_cho_solve)/triangular_solve | solution.py:32
  302.2 2.9 collective-permute-start.5
  305.4 1.0 collective-permute-start.3
  306.4 1.7 collective-permute-done.5
  308.3 3.1 collective-permute-done.3
  314.4 5.8 %cholesky.128 = f32[64,64]{1,0:T(8,128)S(1)} custom-call(f32[64,64]{1,0:T(8,128)S(1)} %fusion.91), custom_call_target="Cholesky" | custom-call | tf_op jit(solution)/shard_map/jit(cholesky)/cholesky | solution.py:30
  321.6 4.9 %custom-call.28 = f32[1,64,64]{1,2,0:T(8,128)S(1)} custom-call(f32[1,64,64]{2,1,0:T(8,128)S(1)} %fusion.86), custom_call_target="InvertDiagBlocksLowerTriangular" | custom-call | tf_op jit(solution)/shard_map/jit(_cho_solve)/triangular_solve | solution.py:32
  (153 shorter events, 32.2 us)
Async XLA Ops:
  7.2 40.8 %all-gather.3.cloned.1.call-start = ((), (), s32[]{:S(2)}) async-start(), calls=%async_computation | async-start | bytes 4718592 | tf_op jit(solution)/shard_map/all_gather | solution.py:79
  7.9 231.5 %all-reduce.2.cloned.1.call-start = ((), (), s32[]{:S(2)}) async-start(), calls=%async_computation.1 | async-start | bytes 8388608 | tf_op jit(solution)/shard_map/psum | solution.py:115
  136.3 0.7 copy-start.1
  136.3 2.3 copy-start.2
  139.4 4.0 %collective-permute-start.1 = (f32[16,64]{0,1:T(8,128)S(1)}, f32[16,64]{0,1:T(8,128)S(1)}, u32[]{:S(2)}, u32[]{:S(2)}) collective-permute-start(f32[16,64]{0,1:T(8,128)S(1)} %select_bitcast_fusion.3), channel_id=1, source_target_pairs={{0,1},{1,0},{2,3},{3,2},{4,5},{5,4},{6,7},{7,6},{8,9},{9,8},{10,11... | collective-permute-start | bytes 12296 | tf_op jit(solution)/shard_map/ppermute | solution.py:13
  144.2 6.4 %collective-permute-start.4 = (f32[16,64]{0,1:T(8,128)S(1)}, f32[16,64]{0,1:T(8,128)S(1)}, u32[]{:S(2)}, u32[]{:S(2)}) collective-permute-start(f32[16,64]{0,1:T(8,128)S(1)} %select_bitcast_fusion.2), channel_id=1, source_target_pairs={{0,2},{1,3},{2,0},{3,1},{4,6},{5,7},{6,4},{7,5},{8,10},{9,11},{10,... | collective-permute-start | bytes 12296 | tf_op jit(solution)/shard_map/ppermute | solution.py:13
  265.0 49.3 %copy-start = (f32[2,64,128]{2,1,0:T(8,128)}, f32[2,64,128]{2,1,0:T(8,128)S(1)}, u32[]{:S(2)}) copy-start(f32[2,64,128]{2,1,0:T(8,128)S(1)} %fusion.75) | copy-start | bytes 196612
  280.9 4.9 %collective-permute-start.2 = (f32[64,256]{1,0:T(8,128)S(1)}, f32[64,256]{1,0:T(8,128)S(1)}, u32[]{:S(2)}, u32[]{:S(2)}) collective-permute-start(f32[64,256]{1,0:T(8,128)S(1)} %fusion.64), channel_id=1, source_target_pairs={{0,1},{1,0},{2,3},{3,2},{4,5},{5,4},{6,7},{7,6},{8,9},{9,8},{10,11... | collective-permute-start | bytes 196616 | tf_op jit(solution)/shard_map/ppermute | solution.py:13
  282.4 4.3 %collective-permute-start = (f32[64,256]{1,0:T(8,128)S(1)}, f32[64,256]{1,0:T(8,128)S(1)}, u32[]{:S(2)}, u32[]{:S(2)}) collective-permute-start(f32[64,256]{1,0:T(8,128)S(1)} %get-tuple-element.116), channel_id=1, source_target_pairs={{0,1},{1,0},{2,3},{3,2},{4,5},{5,4},{6,7},{7,6},{8,9},{9,8},{10,11... | collective-permute-start | bytes 196616 | tf_op jit(solution)/shard_map/ppermute | solution.py:13
  302.2 5.8 %collective-permute-start.5 = (f32[64,256]{1,0:T(8,128)S(1)}, f32[64,256]{1,0:T(8,128)S(1)}, u32[]{:S(2)}, u32[]{:S(2)}) collective-permute-start(f32[64,256]{1,0:T(8,128)S(1)} %fusion.68), channel_id=1, source_target_pairs={{0,2},{1,3},{2,0},{3,1},{4,6},{5,7},{6,4},{7,5},{8,10},{9,11},{10,... | collective-permute-start | bytes 196616 | tf_op jit(solution)/shard_map/ppermute | solution.py:13
  305.4 6.1 %collective-permute-start.3 = (f32[64,256]{1,0:T(8,128)S(1)}, f32[64,256]{1,0:T(8,128)S(1)}, u32[]{:S(2)}, u32[]{:S(2)}) collective-permute-start(f32[64,256]{1,0:T(8,128)S(1)} %get-tuple-element.114), channel_id=1, source_target_pairs={{0,2},{1,3},{2,0},{3,1},{4,6},{5,7},{6,4},{7,5},{8,10},{9,11},{10,... | collective-permute-start | bytes 196616 | tf_op jit(solution)/shard_map/ppermute | solution.py:13
Sparse Core Ops, SparseCore 0:
  9.7 35.7 all-gather.2
  136.5 102.8 all-reduce.1
